TPU v7x, 32 devices: a whole 2x2x4 slice. The times are simulated.
32 devices in a mesh: seg: 16 (over z, x, core), blk: 2 (over y).
Axes of the slice: x: 2, y: 2, z: 4, core: 2. Of those that a mesh axis runs over, the one named last changes fastest.
Arguments:
- queries: bfloat16 [4096, 2048], P(('seg', 'blk')), may hold values from -6 to 6
- keys: bfloat16 [4096, 2048], P(('seg', 'blk')), may hold values from -6 to 6
- values: bfloat16 [4096, 2048], P(('seg', 'blk')), may hold values from -6 to 6
- mid_offset: int32 [16], replicated, may hold values from 0 to 15, as said below
- far_offset: int32 [16], replicated, may hold values from 0 to 127, as said below
Outputs:
- attended: bfloat16 [4096, 2048], P(('seg', 'blk'))
Inputs may be any that keep to these rules, and one draw needn't show every extreme that they name: `mid_offset`: one head has offset 0 and another 16 - 1. `far_offset`: one head has offset 0 and another 128 - 1.
All inputs are finite; a program needn't handle non-finite values.
Results may differ from a plain program's by a relative error of at most 0.0065.
Values may be sent and summed in bfloat16 or wider, within the bound.
A program may use at most 64 MiB of HBM per device.

v0:
```python
import math
import jax
import jax.numpy as jnp
from jax import lax
from jax.sharding import PartitionSpec as P

HEADS = 16
DH = 128
SPAN = 4
MID_RATE = 16
very_low = -1e30


def from_partner(shard, axis, bit):
    return lax.ppermute(shard, axis, [(i, i ^ 1 << bit) for i in range(lax.axis_size(axis))])


def attend_direct(query_rows, key_rows, value_rows):
    score_scale = 1.0 / math.sqrt(query_rows.shape[-1])
    scores = (
        jnp.einsum("qhd,khd->hqk", query_rows, key_rows, preferred_element_type=jnp.float32)
        * score_scale
    )
    row_top = jnp.max(scores, axis=-1)
    weights = jnp.exp(scores - row_top[..., None])
    totals = jnp.sum(weights, axis=-1)
    mixed = jnp.einsum(
        "hqk,khd->qhd", weights.astype(jnp.bfloat16), value_rows, preferred_element_type=jnp.float32
    )
    return (mixed / jnp.transpose(totals)[..., None], jnp.transpose(row_top + jnp.log(totals)))


def online_start(heads, rows, dims):
    return (
        jnp.full((heads, rows), very_low, jnp.float32),
        jnp.zeros((heads, rows), jnp.float32),
        jnp.zeros((heads, rows, dims), jnp.float32),
    )


def online_step(state_now, query_rows, key_rows, value_rows):
    row_top, totals, mixed = state_now
    score_scale = 1.0 / math.sqrt(query_rows.shape[-1])
    scores = (
        jnp.einsum("qhd,khd->hqk", query_rows, key_rows, preferred_element_type=jnp.float32)
        * score_scale
    )
    new_top = jnp.maximum(row_top, jnp.max(scores, axis=-1))
    weights = jnp.exp(scores - new_top[..., None])
    totals = jnp.sum(weights, axis=-1)
    mixed = jnp.einsum(
        "hqk,khd->hqd", weights.astype(jnp.bfloat16), value_rows, preferred_element_type=jnp.float32
    )
    return (new_top, totals, mixed)


def online_finish(state_now):
    row_top, totals, mixed = state_now
    level_out = jnp.transpose(mixed / totals[..., None], (1, 0, 2))
    return (level_out, jnp.transpose(row_top + jnp.log(totals)))


def combine_levels(
    dense_out, dense_lse, mid_out, mid_lse, far_out, far_lse, mid_offset, far_offset
):
    rows = dense_out.shape[0]
    heads = dense_out.shape[1]
    dims = dense_out.shape[2]
    rate = rows // mid_out.shape[0]
    mid_hit = jnp.arange(rate, dtype=jnp.int32)[:, None] == mid_offset[None, :]
    mid_full = jnp.where(mid_hit[None, :, :, None], mid_out[:, None], 0.0).reshape(
        rows, heads, dims
    )
    mid_lse_full = jnp.where(mid_hit[None], mid_lse[:, None, :], very_low).reshape(rows, heads)
    far_hit = jnp.arange(rows, dtype=jnp.int32)[:, None] == far_offset[None, :]
    far_full = jnp.where(far_hit[..., None], far_out[None], 0.0)
    far_lse_full = jnp.where(far_hit, far_lse[None], very_low)
    level_top = jnp.maximum(dense_lse, jnp.maximum(mid_lse_full, far_lse_full))
    dense_weight = jnp.exp(dense_lse - level_top)
    mid_weight = jnp.exp(mid_lse_full - level_top)
    far_weight = jnp.exp(far_lse_full - level_top)
    mixed = (
        dense_weight[..., None] * dense_out
        + mid_weight[..., None] * mid_full
        + far_weight[..., None] * far_full
    )
    mixed = mixed / (dense_weight + mid_weight + far_weight)[..., None]
    return mixed.astype(jnp.bfloat16).reshape(rows, heads * dims)


def on_device(queries, keys, values, mid_offset, far_offset):
    rows = queries.shape[0]
    query_rows = queries.reshape(rows, HEADS, DH)
    key_rows = keys.reshape(rows, HEADS, DH)
    value_rows = values.reshape(rows, HEADS, DH)
    piece_rows = (
        lax.all_gather(keys, "blk", axis=0, tiled=True),
        lax.all_gather(values, "blk", axis=0, tiled=True),
    )
    key_piece = piece_rows[0].reshape(-1, HEADS, DH)
    value_piece = piece_rows[1].reshape(-1, HEADS, DH)
    dense_state = online_step(online_start(HEADS, rows, DH), query_rows, key_piece, value_piece)
    dense_out, dense_lse = online_finish(dense_state)
    mid_select = (jnp.arange(MID_RATE, dtype=jnp.int32)[:, None] == mid_offset[None, :]).astype(
        jnp.bfloat16
    )

    def pick_mid(field):
        shaped = field.reshape(rows // MID_RATE, MID_RATE, HEADS, DH)
        return jnp.einsum(
            "jrhd,rh->jhd", shaped, mid_select, preferred_element_type=jnp.float32
        ).astype(jnp.bfloat16)

    mid_pairs = jnp.stack([pick_mid(key_rows), pick_mid(value_rows)])
    bit_count = SPAN.bit_length() - 1
    mid_pairs = lax.all_gather(mid_pairs, "blk", axis=1, tiled=True)
    for bit_index in range(bit_count):
        partner_rows = from_partner(mid_pairs, "seg", bit_index)
        mid_pairs = jnp.concatenate([mid_pairs, partner_rows], axis=1)
    mid_out, mid_lse = attend_direct(pick_mid(query_rows), mid_pairs[0], mid_pairs[1])
    far_select = (jnp.arange(rows, dtype=jnp.int32)[:, None] == far_offset[None, :]).astype(
        jnp.bfloat16
    )

    def pick_far(field):
        return jnp.einsum(
            "thd,th->hd", field, far_select, preferred_element_type=jnp.float32
        ).astype(jnp.bfloat16)[None]

    far_pairs = jnp.stack([pick_far(key_rows), pick_far(value_rows)])
    far_query = pick_far(query_rows)
    piece_rows = lax.all_gather(far_pairs, ("seg", "blk"), axis=1, tiled=True)
    far_state = online_step(online_start(HEADS, 1, DH), far_query, piece_rows[0], piece_rows[1])
    far_out, far_lse = online_finish(far_state)
    return combine_levels(
        dense_out, dense_lse, mid_out, mid_lse, far_out[0], far_lse[0], mid_offset, far_offset
    )


def solution(mesh):
    return jax.shard_map(
        on_device,
        mesh=mesh,
        in_specs=(
            P(("seg", "blk"), None),
            P(("seg", "blk"), None),
            P(("seg", "blk"), None),
            P(),
            P(),
        ),
        out_specs=P(("seg", "blk"), None),
        check_vma=False,
    )
```

profile of v0, /device:TPU:0, one launch (start us, length us, event | category | flops | bytes accessed | tf_op | source)
XLA Modules:
  0.0 114.1 jit_solution(16395666675392113394)
XLA Ops:
  6.5 2.1 %copy.17 = bf16[128,2048]{0,1:T(8,128)(2,1)} copy(bf16[128,2048]{1,0:T(8,128)(2,1)} %param.6) | data formatting | bytes 1048576 | tf_op args[1]
  8.7 1.2 %copy.49 = bf16[16,8,16,128]{3,2,1,0:T(8,128)(2,1)S(1)} copy(bf16[16,8,16,128]{3,1,2,0:T(8,128)(2,1)} %bitcast.150) | data formatting | bytes 1048576
  10.0 0.1 copy.48
  10.1 0.1 iota_compare_fusion.1
  10.2 0.2 fusion.22
  10.4 0.2 fusion.24
  10.7 5.9 %all_gather.13 = bf16[2,16,16,128]{3,1,2,0:T(8,128)(2,1)S(1)} all-gather(bf16[2,8,16,128]{3,1,2,0:T(8,128)(2,1)S(1)} %pad_maximum_fusion.1), channel_id=1, replica_groups=mesh['seg'=16,'blk'=2] {'blk'}, dimensions={1}, use_global_device_ids=true | all-gather | bytes 196608 | tf_op jit(solution)/shard_map/all_gather | solution.py:116
  16.7 0.2 fusion.12
  16.9 0.3 fusion.15
  17.2 0.3 fusion.18
  17.4 0.1 copy.47
  17.6 0.2 fusion.26
  17.8 71.3 %all_gather.14 = bf16[2,32,16,128]{3,2,1,0:T(8,128)(2,1)S(1)} all-gather(bf16[2,1,16,128]{3,2,1,0:T(8,128)(2,1)S(1)} %pad_maximum_fusion.2), channel_id=1, replica_groups=mesh['seg'=16,'blk'=2] {'seg','blk'}, dimensions={1}, use_global_device_ids=true | all-gather | bytes 270336 | tf_op jit(solution)/shard_map/all_gather | solution.py:132
  89.2 0.2 fusion.32
  89.4 0.1 multiply_reduce_fusion.1
  89.5 0.2 fusion.53
  89.7 0.2 fusion.30
  89.8 0.1 broadcast_divide_fusion
  90.1 0.1 broadcast_in_dim.103
  90.2 6.2 %collective-permute-done.1 = bf16[2,32,16,128]{3,1,2,0:T(8,128)(2,1)S(1)} collective-permute-done((bf16[2,32,16,128]{3,1,2,0:T(8,128)(2,1)S(1)}, bf16[2,32,16,128]{3,1,2,0:T(8,128)(2,1)S(1)}, u32[]{:S(2)}, u32[]{:S(2)}) %collective-permute-start.1) | collective-permute-done | bytes 262176 | tf_op jit(solution)/shard_map/ppermute | solution.py:15
  96.4 0.3 fusion.57
  96.7 0.2 fusion.35
  96.9 0.2 fusion.6
  97.2 0.1 broadcast_in_dim.109
  97.3 1.4 %copy.22 = f32[128,16,128]{0,2,1:T(8,128)} copy(f32[128,16,128]{2,1,0:T(8,128)S(1)} %bitcast.147) | data formatting | bytes 2097152 | tf_op jit(solution)/shard_map/jit(_where)/broadcast_in_dim | solution.py:71
  98.8 0.1 broadcast_in_dim.105
  98.9 1.7 %multiply_reduce_fusion = (f32[16,128]{1,0:T(8,128)S(1)}, f32[16,128,256]{2,1,0:T(8,128)S(1)}) fusion(bf16[256,16,128]{0,2,1:T(8,128)(2,1)} %bitcast.154, bf16[128,2048]{1,0:T(8,128)(2,1)S(1)} %copy-done), kind=kOutput, calls=%fused_computation.1 | convolution fusion | flops 135264256 | bytes 3678208 | tf_op jit(solution)/shard_map/qhd,khd->hqk/dot_general | solution.py:45
  100.7 0.7 fusion.1
  101.4 0.1 add_add_fusion
  101.5 2.3 %copy.20 = bf16[256,2048]{0,1:T(8,128)(2,1)} copy(bf16[256,2048]{1,0:T(8,128)(2,1)} %all-gather.5.cloned.1.call-done) | data formatting | bytes 2097152 | tf_op jit(solution)/shard_map/all_gather | solution.py:98
  103.8 2.4 %divide_convert_fusion = bf16[128,16,128]{0,2,1:T(8,128)(2,1)S(1)} fusion(f32[128,16,128]{0,2,1:T(8,128)} %copy.22, bf16[256,16,128]{0,2,1:T(8,128)(2,1)} %bitcast.155, f32[16,128,256]{2,1,0:T(8,128)S(1)} %get-tuple-element.20, f32[16,128]{1,0:T(8,128)S(1)} %broadcast_maximum_fusion, f32[128,16]{0,1:T(8,128)S(1)} %get-tuple-element.5, ...), kind=kOutput, calls=%fused_computation.12 | convolution fusion | flops 138412032 | bytes 4780032 | tf_op jit(solution)/shard_map/hqk,khd->hqd/dot_general | solution.py:51
  106.2 1.0 copy.23
  (37 shorter events, 0.6 us)
Async XLA Ops:
  6.5 3.4 %copy-start.1 = (bf16[128,2048]{1,0:T(8,128)(2,1)S(1)}, bf16[128,2048]{1,0:T(8,128)(2,1)}, u32[]{:S(2)}) copy-start(bf16[128,2048]{1,0:T(8,128)(2,1)} %param.6) | copy-start | bytes 1572868
  6.5 3.6 %copy-start.4 = (s32[16]{0:T(128)S(1)}, s32[16]{0:T(128)}, u32[]{:S(2)}) copy-start(s32[16]{0:T(128)} %param.8) | copy-start | bytes 196
  6.5 92.4 %all-gather.3.cloned.1.call-start = ((), (), s32[]{:S(2)}) async-start(), calls=%async_computation | async-start | bytes 1572864 | tf_op jit(solution)/shard_map/all_gather | solution.py:97
  8.7 92.8 %all-gather.5.cloned.1.call-start = ((), (), s32[]{:S(2)}) async-start(), calls=%async_computation.1 | async-start | bytes 1572864 | tf_op jit(solution)/shard_map/all_gather | solution.py:98
  8.7 7.9 %copy-start.3 = (s32[16]{0:T(128)S(1)}, s32[16]{0:T(128)}, u32[]{:S(2)}) copy-start(s32[16]{0:T(128)} %param.9) | copy-start | bytes 196
  8.7 8.0 %copy-start.2 = (bf16[128,2048]{1,0:T(8,128)(2,1)S(1)}, bf16[128,2048]{1,0:T(8,128)(2,1)}, u32[]{:S(2)}) copy-start(bf16[128,2048]{1,0:T(8,128)(2,1)} %param.7) | copy-start | bytes 1572868
  10.0 7.2 %copy-start = (bf16[128,2048]{1,0:T(8,128)(2,1)S(1)}, bf16[128,2048]{1,0:T(8,128)(2,1)}, u32[]{:S(2)}) copy-start(bf16[128,2048]{1,0:T(8,128)(2,1)} %param.5) | copy-start | bytes 1572868
  16.6 73.3 %collective-permute-start = (bf16[2,16,16,128]{3,1,2,0:T(8,128)(2,1)S(1)}, bf16[2,16,16,128]{3,1,2,0:T(8,128)(2,1)S(1)}, u32[]{:S(2)}, u32[]{:S(2)}) collective-permute-start(bf16[2,16,16,128]{3,1,2,0:T(8,128)(2,1)S(1)} %all_gather.13), channel_id=1, source_target_pairs={{0,2},{2,0},{4,6},{6,4},{8,10},{10,8},{12,14},{14,12},{16,18},{18,... | collective-permute-start | bytes 393224 | tf_op jit(solution)/shard_map/ppermute | solution.py:15
  90.0 6.4 %collective-permute-start.1 = (bf16[2,32,16,128]{3,1,2,0:T(8,128)(2,1)S(1)}, bf16[2,32,16,128]{3,1,2,0:T(8,128)(2,1)S(1)}, u32[]{:S(2)}, u32[]{:S(2)}) collective-permute-start(bf16[2,32,16,128]{3,1,2,0:T(8,128)(2,1)S(1)} %pad_maximum_fusion), channel_id=1, source_target_pairs={{0,4},{2,6},{4,0},{6,2},{8,12},{10,14},{12,8},{14,10},{16,20},{18,... | collective-permute-start | bytes 786440 | tf_op jit(solution)/shard_map/ppermute | solution.py:15
Sparse Core Ops, SparseCore 0:
  8.9 24.9 all-gather.2
  35.4 22.6 all-gather.4
where the time goes:
time: 114 us
  blocking collectives  77.2 us (68%)
  between operations  13.7 us (12%)
  local copies, waits for them, and re-layouts  8.74 us (8%)
  matrix products  6.45 us (6%)
  waiting for transfers between devices  6.26 us (5%)
  other arithmetic  1.62 us (1%)
    all_gather x1, blocking collectives, on_device(): piece_rows = lax.all_gather(far_pairs, ('seg', 'blk'), axis=1, tiled=True)  71.3 us
    ppermute x2, waiting for transfers between devices, from_partner(): lax.ppermute(shard, axis, [(i, i ^ 1 << bit) for i in range(lax.axis_size...  6.19 us
    all_gather x1, blocking collectives, on_device(): mid_pairs = lax.all_gather(mid_pairs, 'blk', axis=1, tiled=True)  5.89 us
    unnamed x16, local copies, waits for them, and re-layouts  3.61 us
    dot_general x2, matrix products, online_step(): jnp.einsum('hqk,khd->hqd', weights.astype(jnp.bfloat16), value_rows, pref...  2.59 us
  transfers between devices with their start and end apart: 4, of which 1 were waited for; matrix products, arithmetic and copies ran while one was open for 8% of the time, Pallas kernels for 0%

commit v1 on v0

--- a/solution.py
+++ b/solution.py
@@ -9,6 +9,18 @@
 SPAN = 4
 MID_RATE = 16
 very_low = -1e30
+
+
+def doubled_up(x, axis, dim):
+    ways, here = (lax.axis_size(axis), lax.axis_index(axis))
+    grown, reach = (x, 1)
+    while reach < ways:
+        theirs = lax.ppermute(grown, axis, [(d, d ^ reach) for d in range(ways)])
+        mine_first = jnp.concatenate([grown, theirs], axis=dim)
+        theirs_first = jnp.concatenate([theirs, grown], axis=dim)
+        grown = jnp.where(here & reach == 0, mine_first, theirs_first)
+        reach = 2 * reach
+    return grown
 
 
 def from_partner(shard, axis, bit):
@@ -93,10 +105,7 @@
     query_rows = queries.reshape(rows, HEADS, DH)
     key_rows = keys.reshape(rows, HEADS, DH)
     value_rows = values.reshape(rows, HEADS, DH)
-    piece_rows = (
-        lax.all_gather(keys, "blk", axis=0, tiled=True),
-        lax.all_gather(values, "blk", axis=0, tiled=True),
-    )
+    piece_rows = (lax.all_gather(keys, "blk", axis=0, tiled=True), doubled_up(values, "blk", 0))
     key_piece = piece_rows[0].reshape(-1, HEADS, DH)
     value_piece = piece_rows[1].reshape(-1, HEADS, DH)
     dense_state = online_step(online_start(HEADS, rows, DH), query_rows, key_piece, value_piece)

time: 114 us -> 118 us (1.035)
  blocking collectives: 77.2 us -> 80.6 us
  starting transfers between devices: 0.12 us -> 3.04 us
  local copies, waits for them, and re-layouts: 8.74 us -> 6.94 us
    all_gather x1, blocking collectives: 5.89 us -> 9.93 us  [on_device(): mid_pairs = lax.all_gather(mid_pairs, 'blk', axis=1, tiled=True)]
    ppermute x0 -> x1, starting transfers between devices: none -> 2.97 us  [doubled_up(): theirs = lax.ppermute(grown, axis, [(d, d ^ reach) for d in range(ways)])]
    all_gather x1 -> x0, local copies, waits for them, and re-layouts: 2.28 us -> none  [on_device(): lax.all_gather(values, 'blk', axis=0, tiled=True)]
    dot_general x2, matrix products: 2.59 us -> 1.26 us  [online_step(): jnp.einsum('hqk,khd->hqd', weights.astype(jnp.bfloat16), value_rows, pref...]
where the time goes in v1:
time: 118 us
  blocking collectives  80.6 us (68%)
  between operations  13.7 us (12%)
  local copies, waits for them, and re-layouts  6.94 us (6%)
  waiting for transfers between devices  6.22 us (5%)
  matrix products  5.33 us (5%)
  starting transfers between devices  3.04 us (3%)
  other arithmetic  2.3 us (2%)
    all_gather x1, blocking collectives, on_device(): piece_rows = lax.all_gather(far_pairs, ('seg', 'blk'), axis=1, tiled=True)  70.7 us
    all_gather x1, blocking collectives, on_device(): mid_pairs = lax.all_gather(mid_pairs, 'blk', axis=1, tiled=True)  9.93 us
    ppermute x2, waiting for transfers between devices, from_partner(): lax.ppermute(shard, axis, [(i, i ^ 1 << bit) for i in range(lax.axis_size...  6.18 us
    unnamed x16, local copies, waits for them, and re-layouts  3.53 us
    ppermute x1, starting transfers between devices, doubled_up(): theirs = lax.ppermute(grown, axis, [(d, d ^ reach) for d in range(ways)])  2.97 us
  transfers between devices with their start and end apart: 4, of which 1 were waited for; matrix products, arithmetic and copies ran while one was open for 8% of the time, Pallas kernels for 0%

profile of v1, /device:TPU:0, one launch (start us, length us, event | category | flops | bytes accessed | tf_op | source)
XLA Modules:
  0.0 118.2 jit_solution(14463454873200724479)
XLA Ops:
  6.5 3.0 %collective-permute-start.2 = (bf16[128,2048]{1,0:T(8,128)(2,1)}, bf16[128,2048]{1,0:T(8,128)(2,1)S(1)}, u32[]{:S(2)}, u32[]{:S(2)}) collective-permute-start(bf16[128,2048]{1,0:T(8,128)(2,1)} %param.7), channel_id=1, source_target_pairs={{0,1},{1,0},{2,3},{3,2},{4,5},{5,4},{6,7},{7,6},{8,9},{9,8},{10,11... | collective-permute-start | bytes 1572872 | tf_op jit(solution)/shard_map/ppermute | solution.py:18
  9.5 0.7 iota_compare_fusion.1
  10.2 1.1 copy.59
  11.4 1.2 %copy.58 = bf16[16,8,16,128]{3,2,1,0:T(8,128)(2,1)S(1)} copy(bf16[16,8,16,128]{3,1,2,0:T(8,128)(2,1)} %bitcast.143) | data formatting | bytes 1048576
  12.6 0.2 fusion.25
  12.9 0.2 fusion.27
  13.1 9.9 %all_gather.10 = bf16[2,16,16,128]{3,1,2,0:T(8,128)(2,1)S(1)} all-gather(bf16[2,8,16,128]{3,1,2,0:T(8,128)(2,1)S(1)} %pad_maximum_fusion.1), channel_id=1, replica_groups=mesh['seg'=16,'blk'=2] {'blk'}, dimensions={1}, use_global_device_ids=true | all-gather | bytes 196608 | tf_op jit(solution)/shard_map/all_gather | solution.py:125
  23.1 1.0 copy.23
  24.1 0.3 copy.54
  24.5 0.2 fusion.18
  24.7 0.3 fusion.21
  25.0 0.1 copy.57
  25.1 0.2 fusion.29
  25.3 0.4 fusion.43
  25.7 70.7 %all_gather.11 = bf16[2,32,16,128]{3,2,1,0:T(8,128)(2,1)S(1)} all-gather(bf16[2,1,16,128]{3,2,1,0:T(8,128)(2,1)S(1)} %pad_maximum_fusion.2), channel_id=1, replica_groups=mesh['seg'=16,'blk'=2] {'seg','blk'}, dimensions={1}, use_global_device_ids=true | all-gather | bytes 270336 | tf_op jit(solution)/shard_map/all_gather | solution.py:141
  96.4 0.2 fusion.35
  96.6 0.1 multiply_reduce_fusion.1
  96.8 0.2 fusion.57
  96.9 0.2 fusion.33
  97.4 0.1 broadcast_in_dim.103
  97.5 6.2 %collective-permute-done.1 = bf16[2,32,16,128]{3,1,2,0:T(8,128)(2,1)S(1)} collective-permute-done((bf16[2,32,16,128]{3,1,2,0:T(8,128)(2,1)S(1)}, bf16[2,32,16,128]{3,1,2,0:T(8,128)(2,1)S(1)}, u32[]{:S(2)}, u32[]{:S(2)}) %collective-permute-start.1) | collective-permute-done | bytes 262176 | tf_op jit(solution)/shard_map/ppermute | solution.py:27
  103.7 0.3 fusion.62
  104.0 0.2 fusion.38
  104.3 0.1 broadcast_in_dim.105
  104.4 0.2 fusion.6
  104.7 1.4 %copy.31 = f32[128,16,128]{0,2,1:T(8,128)} copy(f32[128,16,128]{2,1,0:T(8,128)S(1)} %bitcast.141) | data formatting | bytes 2097152 | tf_op jit(solution)/shard_map/jit(_where)/broadcast_in_dim | solution.py:83
  106.2 0.3 copy.53
  106.5 1.8 %multiply_reduce_fusion = (f32[16,128]{1,0:T(8,128)S(1)}, f32[16,128,256]{2,1,0:T(8,128)S(1)}) fusion(bf16[256,16,128]{0,2,1:T(8,128)(2,1)} %bitcast.150, bf16[128,2048]{1,0:T(8,128)(2,1)S(1)} %copy-done), kind=kOutput, calls=%fused_computation.1 | convolution fusion | flops 135264256 | bytes 3678208 | tf_op jit(solution)/shard_map/qhd,khd->hqk/dot_general | solution.py:57
  108.3 0.8 fusion.1
  109.1 0.1 add_add_fusion
  109.2 1.1 divide_convert_fusion
  110.3 1.0 copy.32
  (37 shorter events, 0.6 us)
Async XLA Ops:
  6.5 16.5 %copy-start.1 = (bf16[128,2048]{1,0:T(8,128)(2,1)S(1)}, bf16[128,2048]{1,0:T(8,128)(2,1)}, u32[]{:S(2)}) copy-start(bf16[128,2048]{1,0:T(8,128)(2,1)} %param.6) | copy-start | bytes 1572868
  6.5 99.9 %all-gather.2.cloned.1.call-start = ((), (), s32[]{:S(2)}) async-start(), calls=%async_computation | async-start | bytes 1572864 | tf_op jit(solution)/shard_map/all_gather | solution.py:108
  6.5 99.6 %collective-permute-start.2 = (bf16[128,2048]{1,0:T(8,128)(2,1)}, bf16[128,2048]{1,0:T(8,128)(2,1)S(1)}, u32[]{:S(2)}, u32[]{:S(2)}) collective-permute-start(bf16[128,2048]{1,0:T(8,128)(2,1)} %param.7), channel_id=1, source_target_pairs={{0,1},{1,0},{2,3},{3,2},{4,5},{5,4},{6,7},{7,6},{8,9},{9,8},{10,11... | collective-permute-start | bytes 1572872 | tf_op jit(solution)/shard_map/ppermute | solution.py:18
  11.4 12.7 %copy-start.2 = (bf16[128,2048]{1,0:T(8,128)(2,1)S(1)}, bf16[128,2048]{1,0:T(8,128)(2,1)}, u32[]{:S(2)}) copy-start(bf16[128,2048]{1,0:T(8,128)(2,1)} %param.7) | copy-start | bytes 1572868
  12.6 11.8 %copy-start.4 = (s32[16]{0:T(128)S(1)}, s32[16]{0:T(128)}, u32[]{:S(2)}) copy-start(s32[16]{0:T(128)} %param.9) | copy-start | bytes 196
  12.9 11.9 %copy-start = (bf16[128,2048]{1,0:T(8,128)(2,1)S(1)}, bf16[128,2048]{1,0:T(8,128)(2,1)}, u32[]{:S(2)}) copy-start(bf16[128,2048]{1,0:T(8,128)(2,1)} %param.5) | copy-start | bytes 1572868
  23.1 74.1 %collective-permute-start = (bf16[2,16,16,128]{3,1,2,0:T(8,128)(2,1)S(1)}, bf16[2,16,16,128]{3,1,2,0:T(8,128)(2,1)S(1)}, u32[]{:S(2)}, u32[]{:S(2)}) collective-permute-start(bf16[2,16,16,128]{3,1,2,0:T(8,128)(2,1)S(1)} %all_gather.10), channel_id=1, source_target_pairs={{0,2},{2,0},{4,6},{6,4},{8,10},{10,8},{12,14},{14,12},{16,18},{18,... | collective-permute-start | bytes 393224 | tf_op jit(solution)/shard_map/ppermute | solution.py:27
  97.2 6.4 %collective-permute-start.1 = (bf16[2,32,16,128]{3,1,2,0:T(8,128)(2,1)S(1)}, bf16[2,32,16,128]{3,1,2,0:T(8,128)(2,1)S(1)}, u32[]{:S(2)}, u32[]{:S(2)}) collective-permute-start(bf16[2,32,16,128]{3,1,2,0:T(8,128)(2,1)S(1)} %pad_maximum_fusion), channel_id=1, source_target_pairs={{0,4},{2,6},{4,0},{6,2},{8,12},{10,14},{12,8},{14,10},{16,20},{18,... | collective-permute-start | bytes 786440 | tf_op jit(solution)/shard_map/ppermute | solution.py:27
  106.5 2.7 %copy-start.3 = (f32[128,16,128]{0,2,1:T(8,128)S(1)}, f32[128,16,128]{0,2,1:T(8,128)}, u32[]{:S(2)}) copy-start(f32[128,16,128]{0,2,1:T(8,128)} %copy.31) | copy-start | bytes 3145732
Sparse Core Ops, SparseCore 0:
  24.2 24.0 all-gather.1
